TPU v7x, 32 devices: a whole 2x2x4 slice. The times are simulated.
32 devices in a mesh: dp: 4 (over z), rows: 8 (over y, x, core).
Axes of the slice: x: 2, y: 2, z: 4, core: 2. Of those that a mesh axis runs over, the one named last changes fastest.
Arguments:
- inputs: bfloat16 [2, 8192, 9216], P(None, 'dp', 'rows'), may hold values from -21 to 21
- weights: bfloat16 [2, 9216, 4096], P(None, 'rows'), may hold values from -0.0625 to 0.0625
- bias: float32 [2, 4096], P(None, 'rows'), may hold values from -3 to 3
- stitch: float32 [2, 2, 4096], P(None, None, 'rows'), may hold values from 0.2 to 1
- cotangent: bfloat16 [2, 4096, 8192], P(None, 'rows', 'dp'), may hold values from -6 to 6
- valid: int32 [8192], P('dp'), may hold values from 0 to 1, as said below
- size_class: int32 [8192], P('dp'), may hold values from 195 to 227, as said below
Outputs:
- stitched: bfloat16 [2, 4096, 8192], P(None, 'rows', 'dp')
- grad_inputs: bfloat16 [2, 8192, 9216], P(None, 'dp', 'rows')
- grad_weights: float32 [2, 9216, 4096], P(None, 'rows', 'dp')
- grad_bias: float32 [2, 4096], P(None, 'rows')
- grad_stitch: float32 [2, 2, 4096], P(None, None, 'rows')
- rms_values: float32 [3], replicated
Inputs may be any that keep to these rules, and one draw needn't show every extreme that they name: The first image of every aligned block of 2048 images is valid. `size_class`: each entry is 227 or 195.
All inputs are finite; a program needn't handle non-finite values.
Results may differ from a plain program's by a relative error of at most 0.006.
Values may be sent and summed in bfloat16 or wider, within the bound.
A program may use at most 256 MiB of HBM per device.

v0:
```python
import jax
import jax.numpy as jnp
from jax import lax
from jax.sharding import PartitionSpec as P

F = 9216
C = 4096
BLOCK = 128


def chain(own, up):
    size = lax.axis_size("dp")
    here = lax.axis_index("dp")
    got = None
    for step in range(size - 1):
        dest = size - 1 - step + here if up else step - (size - 1) + here
        dest = jnp.clip(dest, 0, size - 1)
        term = lax.dynamic_index_in_dim(own, dest, 0, keepdims=False)
        if got is not None:
            term = (term.astype(jnp.float32) + got.astype(jnp.float32)).astype(jnp.bfloat16)
        pairs = [(z, z + 1) for z in range(step + 1)]
        if not up:
            pairs = [(size - 1 - a, size - 1 - b) for a, b in pairs]
        got = lax.ppermute(term, "dp", pairs)
    return got


def per_device(inputs, weights, bias, stitch, cotangent, valid, size_class):
    rows = lax.axis_size("rows")
    size = lax.axis_size("dp")
    here = lax.axis_index("dp")
    width = inputs.shape[2]
    mine = bias.shape[1]
    step = min(BLOCK, mine)
    blocks = mine // step
    place = lax.iota(jnp.int32, width) % 36
    padded = (place // 6 == 5) | (place % 6 == 5)
    dropped = (size_class == 195)[:, None] & padded[None, :]
    used = jnp.where(dropped[None], jnp.zeros((), jnp.bfloat16), inputs)
    split = weights.reshape(2, width, rows, mine)
    weight_valid = valid.astype(jnp.float32)
    pieces, stitched, grad_bias, grad_stitch, square_pre, square_out = ([], [], [], [], [], [])
    grad_weights = []
    mats = [split[:, :, :, k * step : (k + 1) * step] for k in range(blocks)]
    sums = []
    for k in range(blocks):
        part = jnp.einsum("tfrc,tbf->rctb", mats[k], used, preferred_element_type=jnp.float32)
        sums.append(
            lax.psum_scatter(
                part.reshape(rows * step, 2, -1), "rows", scatter_dimension=0, tiled=True
            )
        )
    for k in range(blocks):
        cut = slice(k * step, (k + 1) * step)
        pre = jnp.transpose(sums[k], (1, 0, 2)) + bias[:, cut, None]
        act = jax.nn.relu(pre)
        mix = stitch[:, :, cut, None]
        out = jnp.sum(mix * act[None], axis=1)
        stitched.append(out.astype(jnp.bfloat16))
        upstream = cotangent[:, cut].astype(jnp.float32) * weight_valid[None, None, :]
        grad_act = jnp.sum(mix * upstream[:, None], axis=0)
        grad_pre = jnp.where(pre > 0, grad_act, 0.0).astype(jnp.bfloat16)
        grad_bias.append(jnp.sum(grad_pre.astype(jnp.float32), axis=2))
        grad_stitch.append(jnp.sum(upstream[:, None] * act[None], axis=3))
        square_pre.append(jnp.sum(weight_valid[None, None, :] * pre * pre))
        square_out.append(jnp.sum(weight_valid[None, None, :] * out * out))
        piece = lax.all_gather(grad_pre, "rows", axis=0)
        pieces.append(piece)
        block = jnp.einsum("tbf,rtcb->rtfc", used, piece, preferred_element_type=jnp.float32)
        block = block.reshape(size, rows // size, 2, width, step)
        own = block.astype(jnp.bfloat16)
        total = lax.dynamic_index_in_dim(block, here, 0, keepdims=False)
        total = total + chain(own, True).astype(jnp.float32) + chain(own, False).astype(jnp.float32)
        grad_weights.append(total)
    total_x = sum(
        (
            jnp.einsum("rtcb,tfrc->tbf", pieces[k], mats[k], preferred_element_type=jnp.float32)
            for k in range(blocks)
        )
    )
    grad_inputs = jnp.where(dropped[None], 0.0, total_x).astype(jnp.bfloat16)
    grad_weights = jnp.stack(grad_weights, axis=0)
    grad_weights = jnp.transpose(grad_weights, (2, 3, 1, 0, 4)).reshape(2, width, -1)
    stitched = jnp.concatenate(stitched, axis=1)
    grad_bias = jnp.concatenate(grad_bias, axis=1)
    grad_stitch = jnp.concatenate(grad_stitch, axis=2)
    used_wide = used.astype(jnp.float32)
    partial_value = jnp.stack(
        [
            jnp.sum(weight_valid[None, :, None] * used_wide * used_wide),
            sum(square_pre),
            sum(square_out),
            jnp.sum(weight_valid),
        ]
    )
    grad_bias, grad_stitch = lax.psum((grad_bias, grad_stitch), "dp")
    totals = lax.psum(partial_value, ("dp", "rows"))
    count = totals[3] / rows
    rms_values = jnp.sqrt(
        jnp.stack(
            [totals[0] / (count * 2 * F), totals[1] / (count * 2 * C), totals[2] / (count * 2 * C)]
        )
    )
    return (stitched, grad_inputs, grad_weights, grad_bias, grad_stitch, rms_values)


def solution(mesh):
    in_specs = (
        P(None, "dp", "rows"),
        P(None, "rows", None),
        P(None, "rows"),
        P(None, None, "rows"),
        P(None, "rows", "dp"),
        P("dp"),
        P("dp"),
    )
    out_specs = (
        P(None, "rows", "dp"),
        P(None, "dp", "rows"),
        P(None, "rows", "dp"),
        P(None, "rows"),
        P(None, None, "rows"),
        P(),
    )
    return jax.shard_map(
        per_device, mesh=mesh, in_specs=in_specs, out_specs=out_specs, check_vma=False
    )
```

profile of v0, /device:TPU:8, one launch (start us, length us, event | category | flops | bytes accessed | tf_op | source)
XLA Modules:
  0.0 1182.2 jit_solution(11360257432043115924)
XLA Ops:
  7.9 24.6 %copy.69 = bf16[2,1152,4096]{1,2,0:T(8,128)(2,1)} copy(bf16[2,1152,4096]{2,1,0:T(8,128)(2,1)} %param.8) | data formatting | bytes 37748736 | tf_op args[1]
  32.6 14.5 %fusion.69 = (bf16[2,1152,8,128]{1,3,2,0:T(8,128)(2,1)}, bf16[2,1152,8,128]{1,3,2,0:T(8,128)(2,1)}, bf16[2,1152,8,128]{1,3,2,0:T(8,128)(2,1)}, bf16[2,1152,8,128]{1,3,2,0:T(8,128)(2,1)}) fusion(bf16[2,1152,8,512]{1,3,2,0:T(8,128)(2,1)} %bitcast.224), kind=kLoop, calls=%fused_computation.159 | loop fusion | bytes 37748736 | tf_op jit(solution)/shard_map/slice | solution.py:44
  48.3 18.3 %convolution_bitcast_fusion.1 = f32[1024,2,2048]{2,0,1:T(8,128)} fusion(bf16[2,1152,1024]{1,2,0:T(8,128)(2,1)} %bitcast.247, bf16[2,2048,1152]{2,1,0:T(8,128)(2,1)} %param.7, pred[2048,1152]{1,0:T(8,128)(4,1)S(1)} %broadcast_and_fusion), kind=kOutput, calls=%fused_computation.25 | convolution fusion | flops 9668395008 | bytes 33292288
  66.7 19.6 %convolution_bitcast_fusion = f32[1024,2,2048]{2,0,1:T(8,128)} fusion(bf16[2,1152,1024]{1,2,0:T(8,128)(2,1)} %bitcast.246, bf16[2,2048,1152]{2,1,0:T(8,128)(2,1)} %param.7, pred[2048,1152]{1,0:T(8,128)(4,1)S(1)} %broadcast_and_fusion), kind=kOutput, calls=%fused_computation.24 | convolution fusion | flops 9668395008 | bytes 33292288
  86.6 20.3 %convolution_bitcast_fusion.2 = f32[1024,2,2048]{2,0,1:T(8,128)} fusion(bf16[2,1152,1024]{1,2,0:T(8,128)(2,1)} %bitcast.248, bf16[2,2048,1152]{2,1,0:T(8,128)(2,1)} %param.7, pred[2048,1152]{1,0:T(8,128)(4,1)S(1)} %broadcast_and_fusion), kind=kOutput, calls=%fused_computation.26 | convolution fusion | flops 9668395008 | bytes 33292288
  106.9 18.3 %convolution_bitcast_fusion.3 = f32[1024,2,2048]{2,0,1:T(8,128)} fusion(bf16[2,1152,1024]{1,2,0:T(8,128)(2,1)} %bitcast.251, bf16[2,2048,1152]{2,1,0:T(8,128)(2,1)} %param.7, pred[2048,1152]{1,0:T(8,128)(4,1)S(1)} %broadcast_and_fusion), kind=kOutput, calls=%fused_computation.27 | convolution fusion | flops 9668395008 | bytes 33292288
  132.2 51.7 %reduce-scatter.9.cloned.1.call-done = f32[128,2,2048]{2,0,1:T(8,128)} async-done(((f32[1024,2,2048]{2,0,1:T(8,128)}), f32[128,2,2048]{2,0,1:T(8,128)}) %reduce-scatter.9.cloned.1.call-update) | async-done | bytes 2097168 | tf_op jit(solution)/shard_map/reduce_scatter | solution.py:49
  183.9 119.5 %reduce-scatter.11.cloned.1.call-done = f32[128,2,2048]{2,0,1:T(8,128)} async-done(((f32[1024,2,2048]{2,0,1:T(8,128)}), f32[128,2,2048]{2,0,1:T(8,128)}) %reduce-scatter.11.cloned.1.call-update) | async-done | bytes 2097168 | tf_op jit(solution)/shard_map/reduce_scatter | solution.py:49
  311.8 111.2 %reduce-scatter.7.cloned.1.call-done = f32[128,2,2048]{2,0,1:T(8,128)} async-done(((f32[1024,2,2048]{2,0,1:T(8,128)}), f32[128,2,2048]{2,0,1:T(8,128)}) %reduce-scatter.7.cloned.1.call-update) | async-done | bytes 2097168 | tf_op jit(solution)/shard_map/reduce_scatter | solution.py:49
  423.0 119.4 %reduce-scatter.5.cloned.1.call-done = f32[128,2,2048]{2,0,1:T(8,128)} async-done(((f32[1024,2,2048]{2,0,1:T(8,128)}), f32[128,2,2048]{2,0,1:T(8,128)}) %reduce-scatter.5.cloned.1.call-update) | async-done | bytes 2097168 | tf_op jit(solution)/shard_map/reduce_scatter | solution.py:49
  575.0 39.5 %psum.23 = f32[4]{0:T(128)S(1)} all-reduce(f32[4]{0:T(128)S(1)} %pad_maximum_fusion.3), channel_id=1, replica_groups=mesh['dp'=4,'rows'=8] {'dp','rows'}, use_global_device_ids=true, to_apply=%region_32.33 | all-reduce | flops 4 | bytes 32 | tf_op jit(solution)/shard_map/psum | solution.py:97
  618.4 14.8 %all-reduce = (f32[2,512]{1,0:T(2,128)}, f32[2,2,512]{2,1,0:T(2,128)}) all-reduce(f32[2,512]{1,0:T(2,128)S(1)} %pad_maximum_fusion.2, f32[2,2,512]{2,1,0:T(2,128)S(1)} %pad_maximum_fusion.1), channel_id=1, replica_groups=mesh['dp'=4,'rows'=8] {'dp'}, use_global_device_ids=true, to_apply=%region_16.17 | all-reduce | flops 3072 | bytes 24576 | tf_op jit(solution)/shard_map/psum | solution.py:96
  637.5 19.4 %fusion.3 = f32[2,8,128,1152]{3,2,1,0:T(8,128)} fusion(bf16[8,2,128,2048]{3,2,1,0:T(8,128)(2,1)} %bitcast.252, bf16[2,2048,1152]{2,1,0:T(8,128)(2,1)} %param.7, pred[2048,1152]{1,0:T(8,128)(4,1)S(1)} %broadcast_and_fusion), kind=kOutput, calls=%fused_computation.8 | convolution fusion | flops 9668395008 | bytes 29622272 | tf_op jit(solution)/shard_map/tbf,rtcb->rtfc/dot_general | solution.py:69
  667.5 18.4 %fusion.9 = f32[2,8,128,1152]{3,2,1,0:T(8,128)} fusion(bf16[8,2,128,2048]{3,2,1,0:T(8,128)(2,1)} %bitcast.254, bf16[2,2048,1152]{2,1,0:T(8,128)(2,1)} %param.7, pred[2048,1152]{1,0:T(8,128)(4,1)S(1)} %broadcast_and_fusion), kind=kOutput, calls=%fused_computation.14 | convolution fusion | flops 9668395008 | bytes 29622272 | tf_op jit(solution)/shard_map/tbf,rtcb->rtfc/dot_general | solution.py:69
  696.1 27.7 %all-gather.11.cloned.1.call-done = bf16[16,128,2048]{2,1,0:T(8,128)(2,1)} async-done(((bf16[2,128,2048]{2,1,0:T(8,128)(2,1)}), bf16[16,128,2048]{2,1,0:T(8,128)(2,1)}) %all-gather.11.cloned.1.call-update) | async-done | bytes 8388624 | tf_op jit(solution)/shard_map/all_gather | solution.py:67
  723.8 18.4 %fusion.7 = f32[2,8,128,1152]{3,2,1,0:T(8,128)} fusion(bf16[8,2,128,2048]{3,2,1,0:T(8,128)(2,1)} %bitcast.258, bf16[2,2048,1152]{2,1,0:T(8,128)(2,1)} %param.7, pred[2048,1152]{1,0:T(8,128)(4,1)S(1)} %broadcast_and_fusion), kind=kOutput, calls=%fused_computation.12 | convolution fusion | flops 9668395008 | bytes 29622272 | tf_op jit(solution)/shard_map/tbf,rtcb->rtfc/dot_general | solution.py:69
  747.6 18.5 %fusion.20 = f32[2,2048,1152,1]{2,1,0,3:T(8,128)} fusion(bf16[8,2,128,2048]{3,2,1,0:T(8,128)(2,1)} %bitcast.255, bf16[2,1152,8,128]{1,3,2,0:T(8,128)(2,1)} %get-tuple-element.36), kind=kOutput, calls=%fused_computation.33 | convolution fusion | flops 9663676416 | bytes 31981568 | tf_op jit(solution)/shard_map/rtcb,tfrc->tbf/dot_general | solution.py:77
  766.1 17.3 %fusion.18 = f32[2,2048,1152,1]{2,1,0,3:T(8,128)} fusion(bf16[8,2,128,2048]{3,2,1,0:T(8,128)(2,1)} %bitcast.259, bf16[2,1152,8,128]{1,3,2,0:T(8,128)(2,1)S(1)} %bitcast.250), kind=kOutput, calls=%fused_computation.31 | convolution fusion | flops 9663676416 | bytes 31981568 | tf_op jit(solution)/shard_map/rtcb,tfrc->tbf/dot_general | solution.py:77
  783.4 18.8 %fusion.16 = f32[2,2048,1152,1]{2,1,0,3:T(8,128)} fusion(bf16[8,2,128,2048]{3,2,1,0:T(8,128)(2,1)} %bitcast.256, bf16[2,1152,8,128]{1,3,2,0:T(8,128)(2,1)} %get-tuple-element.38), kind=kOutput, calls=%fused_computation.29 | convolution fusion | flops 9663676416 | bytes 31981568 | tf_op jit(solution)/shard_map/rtcb,tfrc->tbf/dot_general | solution.py:77
  802.2 28.0 %fusion.2 = bf16[2,2048,1152]{2,1,0:T(8,128)(2,1)} fusion(f32[2,2048,1152,1]{2,1,0,3:T(8,128)} %fusion.16, f32[2,2048,1152,1]{2,1,0,3:T(8,128)} %fusion.18, f32[2,2048,1152,1]{2,1,0,3:T(8,128)} %fusion.20, bf16[8,2,128,2048]{3,2,1,0:T(8,128)(2,1)} %bitcast.253, pred[2048,1152]{1,0:T(8,128)(4,1)S(1)} %broadcast_and_fusion, ...), kind=kOutput, calls=%fused_computation.4 | convolution fusion | flops 9687269376 | bytes 81526784 | tf_op jit(solution)/shard_map/rtcb,tfrc->tbf/dot_general | solution.py:77
  830.1 18.5 %fusion.5 = f32[2,8,128,1152]{3,2,1,0:T(8,128)} fusion(bf16[8,2,128,2048]{3,2,1,0:T(8,128)(2,1)} %bitcast.257, bf16[2,2048,1152]{2,1,0:T(8,128)(2,1)} %param.7, pred[2048,1152]{1,0:T(8,128)(4,1)S(1)} %broadcast_and_fusion), kind=kOutput, calls=%fused_computation.10 | convolution fusion | flops 9668395008 | bytes 29622272 | tf_op jit(solution)/shard_map/tbf,rtcb->rtfc/dot_general | solution.py:69
  865.0 19.2 %collective-permute-done.12 = bf16[2,2,1152,128]{2,3,0,1:T(8,128)(2,1)S(1)} collective-permute-done((bf16[2,2,1152,128]{2,3,0,1:T(8,128)(2,1)S(1)}, bf16[2,2,1152,128]{2,3,0,1:T(8,128)(2,1)S(1)}, u32[]{:S(2)}, u32[]{:S(2)}) %collective-permute-start.12) | collective-permute-done | bytes 1179680 | tf_op jit(solution)/shard_map/ppermute | solution.py:24
  887.3 22.2 %collective-permute-done.19 = bf16[2,2,1152,128]{2,3,0,1:T(8,128)(2,1)S(1)} collective-permute-done((bf16[2,2,1152,128]{2,3,0,1:T(8,128)(2,1)S(1)}, bf16[2,2,1152,128]{2,3,0,1:T(8,128)(2,1)S(1)}, u32[]{:S(2)}, u32[]{:S(2)}) %collective-permute-start.19) | collective-permute-done | bytes 1179680 | tf_op jit(solution)/shard_map/ppermute | solution.py:24
  919.0 15.8 %collective-permute-done.1 = bf16[2,2,1152,128]{2,3,0,1:T(8,128)(2,1)S(1)} collective-permute-done((bf16[2,2,1152,128]{2,3,0,1:T(8,128)(2,1)S(1)}, bf16[2,2,1152,128]{2,3,0,1:T(8,128)(2,1)S(1)}, u32[]{:S(2)}, u32[]{:S(2)}) %collective-permute-start.1) | collective-permute-done | bytes 1179680 | tf_op jit(solution)/shard_map/ppermute | solution.py:24
  942.8 17.4 %collective-permute-done.7 = bf16[2,2,1152,128]{2,3,0,1:T(8,128)(2,1)} collective-permute-done((bf16[2,2,1152,128]{2,3,0,1:T(8,128)(2,1)S(1)}, bf16[2,2,1152,128]{2,3,0,1:T(8,128)(2,1)}, u32[]{:S(2)}, u32[]{:S(2)}) %collective-permute-start.7) | collective-permute-done | bytes 1179680 | tf_op jit(solution)/shard_map/ppermute | solution.py:24
  966.7 18.8 %collective-permute-done.13 = bf16[2,2,1152,128]{2,3,0,1:T(8,128)(2,1)} collective-permute-done((bf16[2,2,1152,128]{2,3,0,1:T(8,128)(2,1)S(1)}, bf16[2,2,1152,128]{2,3,0,1:T(8,128)(2,1)}, u32[]{:S(2)}, u32[]{:S(2)}) %collective-permute-start.13) | collective-permute-done | bytes 1179680 | tf_op jit(solution)/shard_map/ppermute | solution.py:24
  993.4 28.3 %collective-permute-done.10 = bf16[2,2,1152,128]{2,3,0,1:T(8,128)(2,1)S(1)} collective-permute-done((bf16[2,2,1152,128]{2,3,0,1:T(8,128)(2,1)}, bf16[2,2,1152,128]{2,3,0,1:T(8,128)(2,1)S(1)}, u32[]{:S(2)}, u32[]{:S(2)}) %collective-permute-start.10) | collective-permute-done | bytes 1179680 | tf_op jit(solution)/shard_map/ppermute | solution.py:24
  1028.1 18.9 %collective-permute-done.16 = bf16[2,2,1152,128]{2,3,0,1:T(8,128)(2,1)S(1)} collective-permute-done((bf16[2,2,1152,128]{2,3,0,1:T(8,128)(2,1)}, bf16[2,2,1152,128]{2,3,0,1:T(8,128)(2,1)S(1)}, u32[]{:S(2)}, u32[]{:S(2)}) %collective-permute-start.16) | collective-permute-done | bytes 1179680 | tf_op jit(solution)/shard_map/ppermute | solution.py:24
  1053.2 19.1 %collective-permute-done.23 = bf16[2,2,1152,128]{2,3,0,1:T(8,128)(2,1)S(1)} collective-permute-done((bf16[2,2,1152,128]{2,3,0,1:T(8,128)(2,1)S(1)}, bf16[2,2,1152,128]{2,3,0,1:T(8,128)(2,1)S(1)}, u32[]{:S(2)}, u32[]{:S(2)}) %collective-permute-start.23) | collective-permute-done | bytes 1179680 | tf_op jit(solution)/shard_map/ppermute | solution.py:24
  1078.4 19.1 %collective-permute-done.5 = bf16[2,2,1152,128]{2,3,0,1:T(8,128)(2,1)S(1)} collective-permute-done((bf16[2,2,1152,128]{2,3,0,1:T(8,128)(2,1)S(1)}, bf16[2,2,1152,128]{2,3,0,1:T(8,128)(2,1)S(1)}, u32[]{:S(2)}, u32[]{:S(2)}) %collective-permute-start.5) | collective-permute-done | bytes 1179680 | tf_op jit(solution)/shard_map/ppermute | solution.py:24
  1099.7 23.2 %collective-permute-done.11 = bf16[2,2,1152,128]{2,3,0,1:T(8,128)(2,1)S(1)} collective-permute-done((bf16[2,2,1152,128]{2,3,0,1:T(8,128)(2,1)S(1)}, bf16[2,2,1152,128]{2,3,0,1:T(8,128)(2,1)S(1)}, u32[]{:S(2)}, u32[]{:S(2)}) %collective-permute-start.11) | collective-permute-done | bytes 1179680 | tf_op jit(solution)/shard_map/ppermute | solution.py:24
  1123.2 23.3 %collective-permute-done.17 = bf16[2,2,1152,128]{2,3,0,1:T(8,128)(2,1)S(1)} collective-permute-done((bf16[2,2,1152,128]{2,3,0,1:T(8,128)(2,1)S(1)}, bf16[2,2,1152,128]{2,3,0,1:T(8,128)(2,1)S(1)}, u32[]{:S(2)}, u32[]{:S(2)}) %collective-permute-start.17) | collective-permute-done | bytes 1179680 | tf_op jit(solution)/shard_map/ppermute | solution.py:24
  (159 shorter events, 176.8 us)
Async XLA Ops:
  7.2 176.7 %reduce-scatter.9.cloned.1.call-start = ((), (), s32[]{:S(2)}) async-start(), calls=%async_computation.6 | async-start | bytes 18874368 | tf_op jit(solution)/shard_map/reduce_scatter | solution.py:49
  66.6 236.8 %reduce-scatter.11.cloned.1.call-start = ((), (), s32[]{:S(2)}) async-start(), calls=%async_computation.7 | async-start | bytes 18874368 | tf_op jit(solution)/shard_map/reduce_scatter | solution.py:49
  86.3 336.6 %reduce-scatter.7.cloned.1.call-start = ((), (), s32[]{:S(2)}) async-start(), calls=%async_computation.5 | async-start | bytes 18874368 | tf_op jit(solution)/shard_map/reduce_scatter | solution.py:49
  106.9 435.6 %reduce-scatter.5.cloned.1.call-start = ((), (), s32[]{:S(2)}) async-start(), calls=%async_computation.4 | async-start | bytes 18874368 | tf_op jit(solution)/shard_map/reduce_scatter | solution.py:49
  125.3 512.2 %all-gather.15.cloned.1.call-start = ((), (), s32[]{:S(2)}) async-start(), calls=%async_computation.11 | async-start | bytes 9437184 | tf_op jit(solution)/shard_map/all_gather | solution.py:67
  556.4 111.1 %all-gather.9.cloned.1.call-start = ((), (), s32[]{:S(2)}) async-start(), calls=%async_computation.8 | async-start | bytes 9437184 | tf_op jit(solution)/shard_map/all_gather | solution.py:67
  557.0 166.8 %all-gather.11.cloned.1.call-start = ((), (), s32[]{:S(2)}) async-start(), calls=%async_computation.9 | async-start | bytes 9437184 | tf_op jit(solution)/shard_map/all_gather | solution.py:67
  557.7 225.6 %all-gather.13.cloned.1.call-start = ((), (), s32[]{:S(2)}) async-start(), calls=%async_computation.10 | async-start | bytes 9437184 | tf_op jit(solution)/shard_map/all_gather | solution.py:67
  661.0 190.6 %collective-permute-start.18 = (bf16[2,2,1152,128]{2,3,0,1:T(8,128)(2,1)}, bf16[2,2,1152,128]{2,3,0,1:T(8,128)(2,1)}, u32[]{:S(2)}, u32[]{:S(2)}) collective-permute-start(bf16[2,2,1152,128]{2,3,0,1:T(8,128)(2,1)} %get-tuple-element.54), channel_id=1, source_target_pairs={{0,8},{1,9},{2,10},{3,11},{4,12},{5,13},{6,14},{7,15}} | collective-permute-start | bytes 3538952 | tf_op jit(solution)/shard_map/ppermute | solution.py:24
  662.2 224.2 %collective-permute-start.21 = (bf16[2,2,1152,128]{2,3,0,1:T(8,128)(2,1)}, bf16[2,2,1152,128]{2,3,0,1:T(8,128)(2,1)}, u32[]{:S(2)}, u32[]{:S(2)}) collective-permute-start(bf16[2,2,1152,128]{2,3,0,1:T(8,128)(2,1)} %get-tuple-element.55), channel_id=1, source_target_pairs={{24,16},{25,17},{26,18},{27,19},{28,20},{29,21},{30,22},{31,23}} | collective-permute-start | bytes 3538952 | tf_op jit(solution)/shard_map/ppermute | solution.py:24
  693.1 168.2 %collective-permute-start = (bf16[2,2,1152,128]{2,3,0,1:T(8,128)(2,1)}, bf16[2,2,1152,128]{2,3,0,1:T(8,128)(2,1)}, u32[]{:S(2)}, u32[]{:S(2)}) collective-permute-start(bf16[2,2,1152,128]{2,3,0,1:T(8,128)(2,1)} %get-tuple-element.42), channel_id=1, source_target_pairs={{0,8},{1,9},{2,10},{3,11},{4,12},{5,13},{6,14},{7,15}} | collective-permute-start | bytes 3538952 | tf_op jit(solution)/shard_map/ppermute | solution.py:24
  694.4 222.7 %collective-permute-start.3 = (bf16[2,2,1152,128]{2,3,0,1:T(8,128)(2,1)}, bf16[2,2,1152,128]{2,3,0,1:T(8,128)(2,1)}, u32[]{:S(2)}, u32[]{:S(2)}) collective-permute-start(bf16[2,2,1152,128]{2,3,0,1:T(8,128)(2,1)} %get-tuple-element.43), channel_id=1, source_target_pairs={{24,16},{25,17},{26,18},{27,19},{28,20},{29,21},{30,22},{31,23}} | collective-permute-start | bytes 3538952 | tf_op jit(solution)/shard_map/ppermute | solution.py:24
  745.9 109.7 %collective-permute-start.6 = (bf16[2,2,1152,128]{2,3,0,1:T(8,128)(2,1)}, bf16[2,2,1152,128]{2,3,0,1:T(8,128)(2,1)}, u32[]{:S(2)}, u32[]{:S(2)}) collective-permute-start(bf16[2,2,1152,128]{2,3,0,1:T(8,128)(2,1)} %get-tuple-element.46), channel_id=1, source_target_pairs={{0,8},{1,9},{2,10},{3,11},{4,12},{5,13},{6,14},{7,15}} | collective-permute-start | bytes 3538952 | tf_op jit(solution)/shard_map/ppermute | solution.py:24
  851.6 32.7 %collective-permute-start.12 = (bf16[2,2,1152,128]{2,3,0,1:T(8,128)(2,1)S(1)}, bf16[2,2,1152,128]{2,3,0,1:T(8,128)(2,1)S(1)}, u32[]{:S(2)}, u32[]{:S(2)}) collective-permute-start(bf16[2,2,1152,128]{2,3,0,1:T(8,128)(2,1)S(1)} %get-tuple-element.50), channel_id=1, source_target_pairs={{0,8},{1,9},{2,10},{3,11},{4,12},{5,13},{6,14},{7,15}} | collective-permute-start | bytes 3538952 | tf_op jit(solution)/shard_map/ppermute | solution.py:24
  855.5 54.0 %collective-permute-start.19 = (bf16[2,2,1152,128]{2,3,0,1:T(8,128)(2,1)S(1)}, bf16[2,2,1152,128]{2,3,0,1:T(8,128)(2,1)S(1)}, u32[]{:S(2)}, u32[]{:S(2)}) collective-permute-start(bf16[2,2,1152,128]{2,3,0,1:T(8,128)(2,1)S(1)} %fusion.24), channel_id=1, source_target_pairs={{0,8},{8,16},{1,9},{9,17},{2,10},{10,18},{3,11},{11,19},{4,12},{12... | collective-permute-start | bytes 3538952 | tf_op jit(solution)/shard_map/ppermute | solution.py:24
  861.3 80.3 %collective-permute-start.9 = (bf16[2,2,1152,128]{2,3,0,1:T(8,128)(2,1)S(1)}, bf16[2,2,1152,128]{2,3,0,1:T(8,128)(2,1)}, u32[]{:S(2)}, u32[]{:S(2)}) collective-permute-start(bf16[2,2,1152,128]{2,3,0,1:T(8,128)(2,1)S(1)} %get-tuple-element.47), channel_id=1, source_target_pairs={{24,16},{25,17},{26,18},{27,19},{28,20},{29,21},{30,22},{31,23}} | collective-permute-start | bytes 3538952 | tf_op jit(solution)/shard_map/ppermute | solution.py:24
  884.3 50.6 %collective-permute-start.1 = (bf16[2,2,1152,128]{2,3,0,1:T(8,128)(2,1)S(1)}, bf16[2,2,1152,128]{2,3,0,1:T(8,128)(2,1)S(1)}, u32[]{:S(2)}, u32[]{:S(2)}) collective-permute-start(bf16[2,2,1152,128]{2,3,0,1:T(8,128)(2,1)S(1)} %fusion.36), channel_id=1, source_target_pairs={{0,8},{8,16},{1,9},{9,17},{2,10},{10,18},{3,11},{11,19},{4,12},{12... | collective-permute-start | bytes 3538952 | tf_op jit(solution)/shard_map/ppermute | solution.py:24
  886.5 79.0 %collective-permute-start.15 = (bf16[2,2,1152,128]{2,3,0,1:T(8,128)(2,1)S(1)}, bf16[2,2,1152,128]{2,3,0,1:T(8,128)(2,1)S(1)}, u32[]{:S(2)}, u32[]{:S(2)}) collective-permute-start(bf16[2,2,1152,128]{2,3,0,1:T(8,128)(2,1)S(1)} %get-tuple-element.51), channel_id=1, source_target_pairs={{24,16},{25,17},{26,18},{27,19},{28,20},{29,21},{30,22},{31,23}} | collective-permute-start | bytes 3538952 | tf_op jit(solution)/shard_map/ppermute | solution.py:24
  910.6 49.6 %collective-permute-start.7 = (bf16[2,2,1152,128]{2,3,0,1:T(8,128)(2,1)S(1)}, bf16[2,2,1152,128]{2,3,0,1:T(8,128)(2,1)}, u32[]{:S(2)}, u32[]{:S(2)}) collective-permute-start(bf16[2,2,1152,128]{2,3,0,1:T(8,128)(2,1)S(1)} %fusion.32), channel_id=1, source_target_pairs={{0,8},{8,16},{1,9},{9,17},{2,10},{10,18},{3,11},{11,19},{4,12},{12... | collective-permute-start | bytes 3538952 | tf_op jit(solution)/shard_map/ppermute | solution.py:24
  917.1 68.4 %collective-permute-start.13 = (bf16[2,2,1152,128]{2,3,0,1:T(8,128)(2,1)S(1)}, bf16[2,2,1152,128]{2,3,0,1:T(8,128)(2,1)}, u32[]{:S(2)}, u32[]{:S(2)}) collective-permute-start(bf16[2,2,1152,128]{2,3,0,1:T(8,128)(2,1)S(1)} %fusion.28), channel_id=1, source_target_pairs={{0,8},{8,16},{1,9},{9,17},{2,10},{10,18},{3,11},{11,19},{4,12},{12... | collective-permute-start | bytes 3538952 | tf_op jit(solution)/shard_map/ppermute | solution.py:24
  935.9 113.4 %collective-permute-start.20 = (bf16[2,2,1152,128]{2,3,0,1:T(8,128)(2,1)S(1)}, bf16[2,2,1152,128]{2,3,0,1:T(8,128)(2,1)S(1)}, u32[]{:S(2)}, u32[]{:S(2)}) collective-permute-start(bf16[2,2,1152,128]{2,3,0,1:T(8,128)(2,1)S(1)} %get-tuple-element.52), channel_id=1, source_target_pairs={{0,8},{8,16},{16,24},{1,9},{9,17},{17,25},{2,10},{10,18},{18,26},{... | collective-permute-start | bytes 3538952 | tf_op jit(solution)/shard_map/ppermute | solution.py:24
  941.6 48.6 %collective-permute-start.22 = (bf16[2,2,1152,128]{2,3,0,1:T(8,128)(2,1)}, bf16[2,2,1152,128]{2,3,0,1:T(8,128)(2,1)S(1)}, u32[]{:S(2)}, u32[]{:S(2)}) collective-permute-start(bf16[2,2,1152,128]{2,3,0,1:T(8,128)(2,1)} %get-tuple-element.53), channel_id=1, source_target_pairs={{24,16},{16,8},{25,17},{17,9},{26,18},{18,10},{27,19},{19,11},{28,... | collective-permute-start | bytes 3538952 | tf_op jit(solution)/shard_map/ppermute | solution.py:24
  960.2 116.3 %collective-permute-start.2 = (bf16[2,2,1152,128]{2,3,0,1:T(8,128)(2,1)}, bf16[2,2,1152,128]{2,3,0,1:T(8,128)(2,1)S(1)}, u32[]{:S(2)}, u32[]{:S(2)}) collective-permute-start(bf16[2,2,1152,128]{2,3,0,1:T(8,128)(2,1)} %get-tuple-element.40), channel_id=1, source_target_pairs={{0,8},{8,16},{16,24},{1,9},{9,17},{17,25},{2,10},{10,18},{18,26},{... | collective-permute-start | bytes 3538952 | tf_op jit(solution)/shard_map/ppermute | solution.py:24
  965.5 58.4 %collective-permute-start.4 = (bf16[2,2,1152,128]{2,3,0,1:T(8,128)(2,1)}, bf16[2,2,1152,128]{2,3,0,1:T(8,128)(2,1)S(1)}, u32[]{:S(2)}, u32[]{:S(2)}) collective-permute-start(bf16[2,2,1152,128]{2,3,0,1:T(8,128)(2,1)} %get-tuple-element.41), channel_id=1, source_target_pairs={{24,16},{16,8},{25,17},{17,9},{26,18},{18,10},{27,19},{19,11},{28,... | collective-permute-start | bytes 3538952 | tf_op jit(solution)/shard_map/ppermute | solution.py:24
  985.5 36.2 %collective-permute-start.10 = (bf16[2,2,1152,128]{2,3,0,1:T(8,128)(2,1)}, bf16[2,2,1152,128]{2,3,0,1:T(8,128)(2,1)S(1)}, u32[]{:S(2)}, u32[]{:S(2)}) collective-permute-start(bf16[2,2,1152,128]{2,3,0,1:T(8,128)(2,1)} %get-tuple-element.45), channel_id=1, source_target_pairs={{24,16},{16,8},{25,17},{17,9},{26,18},{18,10},{27,19},{19,11},{28,... | collective-permute-start | bytes 3538952 | tf_op jit(solution)/shard_map/ppermute | solution.py:24
  990.2 56.9 %collective-permute-start.16 = (bf16[2,2,1152,128]{2,3,0,1:T(8,128)(2,1)}, bf16[2,2,1152,128]{2,3,0,1:T(8,128)(2,1)S(1)}, u32[]{:S(2)}, u32[]{:S(2)}) collective-permute-start(bf16[2,2,1152,128]{2,3,0,1:T(8,128)(2,1)} %get-tuple-element.49), channel_id=1, source_target_pairs={{24,16},{16,8},{25,17},{17,9},{26,18},{18,10},{27,19},{19,11},{28,... | collective-permute-start | bytes 3538952 | tf_op jit(solution)/shard_map/ppermute | solution.py:24
  1021.7 50.6 %collective-permute-start.23 = (bf16[2,2,1152,128]{2,3,0,1:T(8,128)(2,1)S(1)}, bf16[2,2,1152,128]{2,3,0,1:T(8,128)(2,1)S(1)}, u32[]{:S(2)}, u32[]{:S(2)}) collective-permute-start(bf16[2,2,1152,128]{2,3,0,1:T(8,128)(2,1)S(1)} %fusion.23), channel_id=1, source_target_pairs={{24,16},{16,8},{8,0},{25,17},{17,9},{9,1},{26,18},{18,10},{10,2},{... | collective-permute-start | bytes 3538952 | tf_op jit(solution)/shard_map/ppermute | solution.py:24
  1023.9 75.7 %collective-permute-start.8 = (bf16[2,2,1152,128]{2,3,0,1:T(8,128)(2,1)S(1)}, bf16[2,2,1152,128]{2,3,0,1:T(8,128)(2,1)S(1)}, u32[]{:S(2)}, u32[]{:S(2)}) collective-permute-start(bf16[2,2,1152,128]{2,3,0,1:T(8,128)(2,1)S(1)} %get-tuple-element.44), channel_id=1, source_target_pairs={{0,8},{8,16},{16,24},{1,9},{9,17},{17,25},{2,10},{10,18},{18,26},{... | collective-permute-start | bytes 3538952 | tf_op jit(solution)/shard_map/ppermute | solution.py:24
  1047.0 50.6 %collective-permute-start.5 = (bf16[2,2,1152,128]{2,3,0,1:T(8,128)(2,1)S(1)}, bf16[2,2,1152,128]{2,3,0,1:T(8,128)(2,1)S(1)}, u32[]{:S(2)}, u32[]{:S(2)}) collective-permute-start(bf16[2,2,1152,128]{2,3,0,1:T(8,128)(2,1)S(1)} %fusion.35), channel_id=1, source_target_pairs={{24,16},{16,8},{8,0},{25,17},{17,9},{9,1},{26,18},{18,10},{10,2},{... | collective-permute-start | bytes 3538952 | tf_op jit(solution)/shard_map/ppermute | solution.py:24
  1049.3 74.0 %collective-permute-start.14 = (bf16[2,2,1152,128]{2,3,0,1:T(8,128)(2,1)S(1)}, bf16[2,2,1152,128]{2,3,0,1:T(8,128)(2,1)S(1)}, u32[]{:S(2)}, u32[]{:S(2)}) collective-permute-start(bf16[2,2,1152,128]{2,3,0,1:T(8,128)(2,1)S(1)} %copy-done.14), channel_id=1, source_target_pairs={{0,8},{8,16},{16,24},{1,9},{9,17},{17,25},{2,10},{10,18},{18,26},{... | collective-permute-start | bytes 3538952 | tf_op jit(solution)/shard_map/ppermute | solution.py:24
  1072.3 50.6 %collective-permute-start.11 = (bf16[2,2,1152,128]{2,3,0,1:T(8,128)(2,1)S(1)}, bf16[2,2,1152,128]{2,3,0,1:T(8,128)(2,1)S(1)}, u32[]{:S(2)}, u32[]{:S(2)}) collective-permute-start(bf16[2,2,1152,128]{2,3,0,1:T(8,128)(2,1)S(1)} %fusion.31), channel_id=1, source_target_pairs={{24,16},{16,8},{8,0},{25,17},{17,9},{9,1},{26,18},{18,10},{10,2},{... | collective-permute-start | bytes 3538952 | tf_op jit(solution)/shard_map/ppermute | solution.py:24
  1076.5 70.0 %collective-permute-start.17 = (bf16[2,2,1152,128]{2,3,0,1:T(8,128)(2,1)S(1)}, bf16[2,2,1152,128]{2,3,0,1:T(8,128)(2,1)S(1)}, u32[]{:S(2)}, u32[]{:S(2)}) collective-permute-start(bf16[2,2,1152,128]{2,3,0,1:T(8,128)(2,1)S(1)} %fusion.27), channel_id=1, source_target_pairs={{24,16},{16,8},{8,0},{25,17},{17,9},{9,1},{26,18},{18,10},{10,2},{... | collective-permute-start | bytes 3538952 | tf_op jit(solution)/shard_map/ppermute | solution.py:24
  (27 other events, 652.0 us)
Sparse Core Ops, SparseCore 0:
  66.8 117.1 reduce-scatter.8
  187.5 115.9 reduce-scatter.10
  307.0 115.9 reduce-scatter.6
  426.4 115.9 reduce-scatter.4
  556.5 54.6 all-gather.14
  613.0 54.4 all-gather.8
  669.3 54.3 all-gather.10
  725.7 54.3 all-gather.12
where the time goes:
time: 1190 us; the launch traced here: 1180 us
  waiting for transfers between devices  660 us (55%)
  matrix products  234 us (20%)
  local copies, waits for them, and re-layouts  83.1 us (7%)
  other arithmetic  80.9 us (7%)
  blocking collectives  54.4 us (5%)
  starting transfers between devices  46.9 us (4%)
  between operations  23.4 us (2%)
    reduce_scatter x4, waiting for transfers between devices, per_device(): lax.psum_scatter(part.reshape(rows * step, 2, -1), 'rows', scatter_dimens...  402 us
    ppermute x24, waiting for transfers between devices, chain(): got = lax.ppermute(term, 'dp', pairs)  225 us
    dot_general x4, matrix products, per_device(): jnp.einsum('rtcb,tfrc->tbf', pieces[k], mats[k], preferred_element_type=j...  82.5 us
    unnamed x4, matrix products  76.5 us
    dot_general x4, matrix products, per_device(): jnp.einsum('tbf,rtcb->rtfc', used, piece, preferred_element_type=jnp.floa...  74.6 us
    ppermute x24, starting transfers between devices, chain(): got = lax.ppermute(term, 'dp', pairs)  45.8 us
    psum x1, blocking collectives, per_device(): totals = lax.psum(partial_value, ('dp', 'rows'))  39.5 us
    unnamed x55, local copies, waits for them, and re-layouts  31.3 us
  transfers between devices with their start and end apart: 32, of which 17 were waited for; matrix products, arithmetic and copies ran while one was open for 25% of the time, Pallas kernels for 0%

commit v1 on v0

--- a/solution.py
+++ b/solution.py
@@ -94,7 +94,7 @@
         ]
     )
     grad_bias, grad_stitch = lax.psum((grad_bias, grad_stitch), "dp")
-    totals = lax.psum(partial_value, ("dp", "rows"))
+    totals = lax.psum(lax.psum(partial_value, "rows"), "dp")
     count = totals[3] / rows
     rms_values = jnp.sqrt(
         jnp.stack(

time: 1190 us -> 1190 us (level)
  waiting for transfers between devices: 660 us -> 686 us
  blocking collectives: 54.4 us -> 28.5 us
    psum x1, blocking collectives: 39.5 us -> 12.8 us  [per_device(): totals = lax.psum(lax.psum(partial_value, 'rows'), 'dp')]
    all_gather x4, waiting for transfers between devices: 31 us -> 57.4 us  [per_device(): piece = lax.all_gather(grad_pre, 'rows', axis=0)]
where the time goes in v1:
time: 1190 us; the launch traced here: 1180 us
  waiting for transfers between devices  686 us (58%)
  matrix products  233 us (20%)
  local copies, waits for them, and re-layouts  83.1 us (7%)
  other arithmetic  80.9 us (7%)
  starting transfers between devices  46.9 us (4%)
  blocking collectives  28.5 us (2%)
  between operations  23.3 us (2%)
    reduce_scatter x4, waiting for transfers between devices, per_device(): lax.psum_scatter(part.reshape(rows * step, 2, -1), 'rows', scatter_dimens...  402 us
    ppermute x24, waiting for transfers between devices, chain(): got = lax.ppermute(term, 'dp', pairs)  225 us
    dot_general x4, matrix products, per_device(): jnp.einsum('rtcb,tfrc->tbf', pieces[k], mats[k], preferred_element_type=j...  82.5 us
    unnamed x4, matrix products  76.5 us
    dot_general x4, matrix products, per_device(): jnp.einsum('tbf,rtcb->rtfc', used, piece, preferred_element_type=jnp.floa...  73.7 us
    all_gather x4, waiting for transfers between devices, per_device(): piece = lax.all_gather(grad_pre, 'rows', axis=0)  57.4 us
    ppermute x24, starting transfers between devices, chain(): got = lax.ppermute(term, 'dp', pairs)  45.8 us
    unnamed x55, local copies, waits for them, and re-layouts  31.3 us
  transfers between devices with their start and end apart: 32, of which 17 were waited for; matrix products, arithmetic and copies ran while one was open for 25% of the time, Pallas kernels for 0%

profile of v1, /device:TPU:8, one launch (start us, length us, event | category | flops | bytes accessed | tf_op | source)
XLA Modules:
  0.0 1181.8 jit_solution(7154522752120335670)
XLA Ops:
  7.9 24.6 %copy.69 = bf16[2,1152,4096]{1,2,0:T(8,128)(2,1)} copy(bf16[2,1152,4096]{2,1,0:T(8,128)(2,1)} %param.8) | data formatting | bytes 37748736 | tf_op args[1]
  32.6 14.5 %fusion.69 = (bf16[2,1152,8,128]{1,3,2,0:T(8,128)(2,1)}, bf16[2,1152,8,128]{1,3,2,0:T(8,128)(2,1)}, bf16[2,1152,8,128]{1,3,2,0:T(8,128)(2,1)}, bf16[2,1152,8,128]{1,3,2,0:T(8,128)(2,1)}) fusion(bf16[2,1152,8,512]{1,3,2,0:T(8,128)(2,1)} %bitcast.224), kind=kLoop, calls=%fused_computation.159 | loop fusion | bytes 37748736 | tf_op jit(solution)/shard_map/slice | solution.py:44
  48.3 18.3 %convolution_bitcast_fusion.1 = f32[1024,2,2048]{2,0,1:T(8,128)} fusion(bf16[2,1152,1024]{1,2,0:T(8,128)(2,1)} %bitcast.247, bf16[2,2048,1152]{2,1,0:T(8,128)(2,1)} %param.7, pred[2048,1152]{1,0:T(8,128)(4,1)S(1)} %broadcast_and_fusion), kind=kOutput, calls=%fused_computation.25 | convolution fusion | flops 9668395008 | bytes 33292288
  66.7 19.6 %convolution_bitcast_fusion = f32[1024,2,2048]{2,0,1:T(8,128)} fusion(bf16[2,1152,1024]{1,2,0:T(8,128)(2,1)} %bitcast.246, bf16[2,2048,1152]{2,1,0:T(8,128)(2,1)} %param.7, pred[2048,1152]{1,0:T(8,128)(4,1)S(1)} %broadcast_and_fusion), kind=kOutput, calls=%fused_computation.24 | convolution fusion | flops 9668395008 | bytes 33292288
  86.6 20.3 %convolution_bitcast_fusion.2 = f32[1024,2,2048]{2,0,1:T(8,128)} fusion(bf16[2,1152,1024]{1,2,0:T(8,128)(2,1)} %bitcast.248, bf16[2,2048,1152]{2,1,0:T(8,128)(2,1)} %param.7, pred[2048,1152]{1,0:T(8,128)(4,1)S(1)} %broadcast_and_fusion), kind=kOutput, calls=%fused_computation.26 | convolution fusion | flops 9668395008 | bytes 33292288
  106.9 18.3 %convolution_bitcast_fusion.3 = f32[1024,2,2048]{2,0,1:T(8,128)} fusion(bf16[2,1152,1024]{1,2,0:T(8,128)(2,1)} %bitcast.251, bf16[2,2048,1152]{2,1,0:T(8,128)(2,1)} %param.7, pred[2048,1152]{1,0:T(8,128)(4,1)S(1)} %broadcast_and_fusion), kind=kOutput, calls=%fused_computation.27 | convolution fusion | flops 9668395008 | bytes 33292288
  132.2 51.7 %reduce-scatter.9.cloned.1.call-done = f32[128,2,2048]{2,0,1:T(8,128)} async-done(((f32[1024,2,2048]{2,0,1:T(8,128)}), f32[128,2,2048]{2,0,1:T(8,128)}) %reduce-scatter.9.cloned.1.call-update) | async-done | bytes 2097168 | tf_op jit(solution)/shard_map/reduce_scatter | solution.py:49
  183.9 119.5 %reduce-scatter.11.cloned.1.call-done = f32[128,2,2048]{2,0,1:T(8,128)} async-done(((f32[1024,2,2048]{2,0,1:T(8,128)}), f32[128,2,2048]{2,0,1:T(8,128)}) %reduce-scatter.11.cloned.1.call-update) | async-done | bytes 2097168 | tf_op jit(solution)/shard_map/reduce_scatter | solution.py:49
  311.8 111.2 %reduce-scatter.7.cloned.1.call-done = f32[128,2,2048]{2,0,1:T(8,128)} async-done(((f32[1024,2,2048]{2,0,1:T(8,128)}), f32[128,2,2048]{2,0,1:T(8,128)}) %reduce-scatter.7.cloned.1.call-update) | async-done | bytes 2097168 | tf_op jit(solution)/shard_map/reduce_scatter | solution.py:49
  423.0 119.4 %reduce-scatter.5.cloned.1.call-done = f32[128,2,2048]{2,0,1:T(8,128)} async-done(((f32[1024,2,2048]{2,0,1:T(8,128)}), f32[128,2,2048]{2,0,1:T(8,128)}) %reduce-scatter.5.cloned.1.call-update) | async-done | bytes 2097168 | tf_op jit(solution)/shard_map/reduce_scatter | solution.py:49
  587.8 15.8 %all-reduce = (f32[2,512]{1,0:T(2,128)}, f32[2,2,512]{2,1,0:T(2,128)}, f32[4]{0:T(128)S(1)}) all-reduce(f32[2,512]{1,0:T(2,128)S(1)} %pad_maximum_fusion.2, f32[2,2,512]{2,1,0:T(2,128)S(1)} %pad_maximum_fusion.1, f32[4]{0:T(128)S(1)} %psum.30), channel_id=1, replica_groups=mesh['dp'=4,'rows'=8] {'dp'}, use_global_device_ids=true, to_apply=%region_16.17 | all-reduce | flops 3076 | bytes 24608 | tf_op jit(solution)/shard_map/psum | solution.py:96
  611.6 18.4 %fusion.3 = f32[2,8,128,1152]{3,2,1,0:T(8,128)} fusion(bf16[8,2,128,2048]{3,2,1,0:T(8,128)(2,1)} %bitcast.252, bf16[2,2048,1152]{2,1,0:T(8,128)(2,1)} %param.7, pred[2048,1152]{1,0:T(8,128)(4,1)S(1)} %broadcast_and_fusion), kind=kOutput, calls=%fused_computation.8 | convolution fusion | flops 9668395008 | bytes 29622272 | tf_op jit(solution)/shard_map/tbf,rtcb->rtfc/dot_general | solution.py:69
  637.3 29.7 %all-gather.9.cloned.1.call-done = bf16[16,128,2048]{2,1,0:T(8,128)(2,1)} async-done(((bf16[2,128,2048]{2,1,0:T(8,128)(2,1)}), bf16[16,128,2048]{2,1,0:T(8,128)(2,1)}) %all-gather.9.cloned.1.call-update) | async-done | bytes 8388624 | tf_op jit(solution)/shard_map/all_gather | solution.py:67
  667.1 18.4 %fusion.9 = f32[2,8,128,1152]{3,2,1,0:T(8,128)} fusion(bf16[8,2,128,2048]{3,2,1,0:T(8,128)(2,1)} %bitcast.254, bf16[2,2048,1152]{2,1,0:T(8,128)(2,1)} %param.7, pred[2048,1152]{1,0:T(8,128)(4,1)S(1)} %broadcast_and_fusion), kind=kOutput, calls=%fused_computation.14 | convolution fusion | flops 9668395008 | bytes 29622272 | tf_op jit(solution)/shard_map/tbf,rtcb->rtfc/dot_general | solution.py:69
  695.7 27.7 %all-gather.11.cloned.1.call-done = bf16[16,128,2048]{2,1,0:T(8,128)(2,1)} async-done(((bf16[2,128,2048]{2,1,0:T(8,128)(2,1)}), bf16[16,128,2048]{2,1,0:T(8,128)(2,1)}) %all-gather.11.cloned.1.call-update) | async-done | bytes 8388624 | tf_op jit(solution)/shard_map/all_gather | solution.py:67
  723.4 18.4 %fusion.7 = f32[2,8,128,1152]{3,2,1,0:T(8,128)} fusion(bf16[8,2,128,2048]{3,2,1,0:T(8,128)(2,1)} %bitcast.258, bf16[2,2048,1152]{2,1,0:T(8,128)(2,1)} %param.7, pred[2048,1152]{1,0:T(8,128)(4,1)S(1)} %broadcast_and_fusion), kind=kOutput, calls=%fused_computation.12 | convolution fusion | flops 9668395008 | bytes 29622272 | tf_op jit(solution)/shard_map/tbf,rtcb->rtfc/dot_general | solution.py:69
  747.2 18.5 %fusion.20 = f32[2,2048,1152,1]{2,1,0,3:T(8,128)} fusion(bf16[8,2,128,2048]{3,2,1,0:T(8,128)(2,1)} %bitcast.255, bf16[2,1152,8,128]{1,3,2,0:T(8,128)(2,1)} %get-tuple-element.37), kind=kOutput, calls=%fused_computation.33 | convolution fusion | flops 9663676416 | bytes 31981568 | tf_op jit(solution)/shard_map/rtcb,tfrc->tbf/dot_general | solution.py:77
  765.7 17.2 %fusion.18 = f32[2,2048,1152,1]{2,1,0,3:T(8,128)} fusion(bf16[8,2,128,2048]{3,2,1,0:T(8,128)(2,1)} %bitcast.259, bf16[2,1152,8,128]{1,3,2,0:T(8,128)(2,1)S(1)} %bitcast.250), kind=kOutput, calls=%fused_computation.31 | convolution fusion | flops 9663676416 | bytes 31981568 | tf_op jit(solution)/shard_map/rtcb,tfrc->tbf/dot_general | solution.py:77
  783.0 18.8 %fusion.16 = f32[2,2048,1152,1]{2,1,0,3:T(8,128)} fusion(bf16[8,2,128,2048]{3,2,1,0:T(8,128)(2,1)} %bitcast.256, bf16[2,1152,8,128]{1,3,2,0:T(8,128)(2,1)} %get-tuple-element.39), kind=kOutput, calls=%fused_computation.29 | convolution fusion | flops 9663676416 | bytes 31981568 | tf_op jit(solution)/shard_map/rtcb,tfrc->tbf/dot_general | solution.py:77
  801.8 28.0 %fusion.2 = bf16[2,2048,1152]{2,1,0:T(8,128)(2,1)} fusion(f32[2,2048,1152,1]{2,1,0,3:T(8,128)} %fusion.16, f32[2,2048,1152,1]{2,1,0,3:T(8,128)} %fusion.18, f32[2,2048,1152,1]{2,1,0,3:T(8,128)} %fusion.20, bf16[8,2,128,2048]{3,2,1,0:T(8,128)(2,1)} %bitcast.253, pred[2048,1152]{1,0:T(8,128)(4,1)S(1)} %broadcast_and_fusion, ...), kind=kOutput, calls=%fused_computation.4 | convolution fusion | flops 9687269376 | bytes 81526784 | tf_op jit(solution)/shard_map/rtcb,tfrc->tbf/dot_general | solution.py:77
  829.8 18.5 %fusion.5 = f32[2,8,128,1152]{3,2,1,0:T(8,128)} fusion(bf16[8,2,128,2048]{3,2,1,0:T(8,128)(2,1)} %bitcast.257, bf16[2,2048,1152]{2,1,0:T(8,128)(2,1)} %param.7, pred[2048,1152]{1,0:T(8,128)(4,1)S(1)} %broadcast_and_fusion), kind=kOutput, calls=%fused_computation.10 | convolution fusion | flops 9668395008 | bytes 29622272 | tf_op jit(solution)/shard_map/tbf,rtcb->rtfc/dot_general | solution.py:69
  864.7 19.2 %collective-permute-done.12 = bf16[2,2,1152,128]{2,3,0,1:T(8,128)(2,1)S(1)} collective-permute-done((bf16[2,2,1152,128]{2,3,0,1:T(8,128)(2,1)S(1)}, bf16[2,2,1152,128]{2,3,0,1:T(8,128)(2,1)S(1)}, u32[]{:S(2)}, u32[]{:S(2)}) %collective-permute-start.12) | collective-permute-done | bytes 1179680 | tf_op jit(solution)/shard_map/ppermute | solution.py:24
  887.0 22.2 %collective-permute-done.19 = bf16[2,2,1152,128]{2,3,0,1:T(8,128)(2,1)S(1)} collective-permute-done((bf16[2,2,1152,128]{2,3,0,1:T(8,128)(2,1)S(1)}, bf16[2,2,1152,128]{2,3,0,1:T(8,128)(2,1)S(1)}, u32[]{:S(2)}, u32[]{:S(2)}) %collective-permute-start.19) | collective-permute-done | bytes 1179680 | tf_op jit(solution)/shard_map/ppermute | solution.py:24
  918.7 15.8 %collective-permute-done.1 = bf16[2,2,1152,128]{2,3,0,1:T(8,128)(2,1)S(1)} collective-permute-done((bf16[2,2,1152,128]{2,3,0,1:T(8,128)(2,1)S(1)}, bf16[2,2,1152,128]{2,3,0,1:T(8,128)(2,1)S(1)}, u32[]{:S(2)}, u32[]{:S(2)}) %collective-permute-start.1) | collective-permute-done | bytes 1179680 | tf_op jit(solution)/shard_map/ppermute | solution.py:24
  942.5 17.4 %collective-permute-done.7 = bf16[2,2,1152,128]{2,3,0,1:T(8,128)(2,1)} collective-permute-done((bf16[2,2,1152,128]{2,3,0,1:T(8,128)(2,1)S(1)}, bf16[2,2,1152,128]{2,3,0,1:T(8,128)(2,1)}, u32[]{:S(2)}, u32[]{:S(2)}) %collective-permute-start.7) | collective-permute-done | bytes 1179680 | tf_op jit(solution)/shard_map/ppermute | solution.py:24
  966.4 18.8 %collective-permute-done.13 = bf16[2,2,1152,128]{2,3,0,1:T(8,128)(2,1)} collective-permute-done((bf16[2,2,1152,128]{2,3,0,1:T(8,128)(2,1)S(1)}, bf16[2,2,1152,128]{2,3,0,1:T(8,128)(2,1)}, u32[]{:S(2)}, u32[]{:S(2)}) %collective-permute-start.13) | collective-permute-done | bytes 1179680 | tf_op jit(solution)/shard_map/ppermute | solution.py:24
  993.0 28.3 %collective-permute-done.10 = bf16[2,2,1152,128]{2,3,0,1:T(8,128)(2,1)S(1)} collective-permute-done((bf16[2,2,1152,128]{2,3,0,1:T(8,128)(2,1)}, bf16[2,2,1152,128]{2,3,0,1:T(8,128)(2,1)S(1)}, u32[]{:S(2)}, u32[]{:S(2)}) %collective-permute-start.10) | collective-permute-done | bytes 1179680 | tf_op jit(solution)/shard_map/ppermute | solution.py:24
  1027.8 18.9 %collective-permute-done.16 = bf16[2,2,1152,128]{2,3,0,1:T(8,128)(2,1)S(1)} collective-permute-done((bf16[2,2,1152,128]{2,3,0,1:T(8,128)(2,1)}, bf16[2,2,1152,128]{2,3,0,1:T(8,128)(2,1)S(1)}, u32[]{:S(2)}, u32[]{:S(2)}) %collective-permute-start.16) | collective-permute-done | bytes 1179680 | tf_op jit(solution)/shard_map/ppermute | solution.py:24
  1052.8 19.1 %collective-permute-done.23 = bf16[2,2,1152,128]{2,3,0,1:T(8,128)(2,1)S(1)} collective-permute-done((bf16[2,2,1152,128]{2,3,0,1:T(8,128)(2,1)S(1)}, bf16[2,2,1152,128]{2,3,0,1:T(8,128)(2,1)S(1)}, u32[]{:S(2)}, u32[]{:S(2)}) %collective-permute-start.23) | collective-permute-done | bytes 1179680 | tf_op jit(solution)/shard_map/ppermute | solution.py:24
  1078.1 19.1 %collective-permute-done.5 = bf16[2,2,1152,128]{2,3,0,1:T(8,128)(2,1)S(1)} collective-permute-done((bf16[2,2,1152,128]{2,3,0,1:T(8,128)(2,1)S(1)}, bf16[2,2,1152,128]{2,3,0,1:T(8,128)(2,1)S(1)}, u32[]{:S(2)}, u32[]{:S(2)}) %collective-permute-start.5) | collective-permute-done | bytes 1179680 | tf_op jit(solution)/shard_map/ppermute | solution.py:24
  1099.3 23.2 %collective-permute-done.11 = bf16[2,2,1152,128]{2,3,0,1:T(8,128)(2,1)S(1)} collective-permute-done((bf16[2,2,1152,128]{2,3,0,1:T(8,128)(2,1)S(1)}, bf16[2,2,1152,128]{2,3,0,1:T(8,128)(2,1)S(1)}, u32[]{:S(2)}, u32[]{:S(2)}) %collective-permute-start.11) | collective-permute-done | bytes 1179680 | tf_op jit(solution)/shard_map/ppermute | solution.py:24
  1122.9 23.2 %collective-permute-done.17 = bf16[2,2,1152,128]{2,3,0,1:T(8,128)(2,1)S(1)} collective-permute-done((bf16[2,2,1152,128]{2,3,0,1:T(8,128)(2,1)S(1)}, bf16[2,2,1152,128]{2,3,0,1:T(8,128)(2,1)S(1)}, u32[]{:S(2)}, u32[]{:S(2)}) %collective-permute-start.17) | collective-permute-done | bytes 1179680 | tf_op jit(solution)/shard_map/ppermute | solution.py:24
  (159 shorter events, 186.2 us)
Async XLA Ops:
  7.2 176.7 %reduce-scatter.9.cloned.1.call-start = ((), (), s32[]{:S(2)}) async-start(), calls=%async_computation.6 | async-start | bytes 18874368 | tf_op jit(solution)/shard_map/reduce_scatter | solution.py:49
  66.6 236.8 %reduce-scatter.11.cloned.1.call-start = ((), (), s32[]{:S(2)}) async-start(), calls=%async_computation.7 | async-start | bytes 18874368 | tf_op jit(solution)/shard_map/reduce_scatter | solution.py:49
  86.3 336.6 %reduce-scatter.7.cloned.1.call-start = ((), (), s32[]{:S(2)}) async-start(), calls=%async_computation.5 | async-start | bytes 18874368 | tf_op jit(solution)/shard_map/reduce_scatter | solution.py:49
  106.9 435.6 %reduce-scatter.5.cloned.1.call-start = ((), (), s32[]{:S(2)}) async-start(), calls=%async_computation.4 | async-start | bytes 18874368 | tf_op jit(solution)/shard_map/reduce_scatter | solution.py:49
  125.3 486.4 %all-gather.15.cloned.1.call-start = ((), (), s32[]{:S(2)}) async-start(), calls=%async_computation.11 | async-start | bytes 9437184 | tf_op jit(solution)/shard_map/all_gather | solution.py:67
  556.4 110.7 %all-gather.9.cloned.1.call-start = ((), (), s32[]{:S(2)}) async-start(), calls=%async_computation.8 | async-start | bytes 9437184 | tf_op jit(solution)/shard_map/all_gather | solution.py:67
  557.0 166.4 %all-gather.11.cloned.1.call-start = ((), (), s32[]{:S(2)}) async-start(), calls=%async_computation.9 | async-start | bytes 9437184 | tf_op jit(solution)/shard_map/all_gather | solution.py:67
  557.7 225.3 %all-gather.13.cloned.1.call-start = ((), (), s32[]{:S(2)}) async-start(), calls=%async_computation.10 | async-start | bytes 9437184 | tf_op jit(solution)/shard_map/all_gather | solution.py:67
  634.2 217.0 %collective-permute-start.18 = (bf16[2,2,1152,128]{2,3,0,1:T(8,128)(2,1)}, bf16[2,2,1152,128]{2,3,0,1:T(8,128)(2,1)}, u32[]{:S(2)}, u32[]{:S(2)}) collective-permute-start(bf16[2,2,1152,128]{2,3,0,1:T(8,128)(2,1)} %get-tuple-element.55), channel_id=1, source_target_pairs={{0,8},{1,9},{2,10},{3,11},{4,12},{5,13},{6,14},{7,15}} | collective-permute-start | bytes 3538952 | tf_op jit(solution)/shard_map/ppermute | solution.py:24
  635.5 250.6 %collective-permute-start.21 = (bf16[2,2,1152,128]{2,3,0,1:T(8,128)(2,1)}, bf16[2,2,1152,128]{2,3,0,1:T(8,128)(2,1)}, u32[]{:S(2)}, u32[]{:S(2)}) collective-permute-start(bf16[2,2,1152,128]{2,3,0,1:T(8,128)(2,1)} %get-tuple-element.56), channel_id=1, source_target_pairs={{24,16},{25,17},{26,18},{27,19},{28,20},{29,21},{30,22},{31,23}} | collective-permute-start | bytes 3538952 | tf_op jit(solution)/shard_map/ppermute | solution.py:24
  692.7 168.2 %collective-permute-start = (bf16[2,2,1152,128]{2,3,0,1:T(8,128)(2,1)}, bf16[2,2,1152,128]{2,3,0,1:T(8,128)(2,1)}, u32[]{:S(2)}, u32[]{:S(2)}) collective-permute-start(bf16[2,2,1152,128]{2,3,0,1:T(8,128)(2,1)} %get-tuple-element.43), channel_id=1, source_target_pairs={{0,8},{1,9},{2,10},{3,11},{4,12},{5,13},{6,14},{7,15}} | collective-permute-start | bytes 3538952 | tf_op jit(solution)/shard_map/ppermute | solution.py:24
  694.0 222.7 %collective-permute-start.3 = (bf16[2,2,1152,128]{2,3,0,1:T(8,128)(2,1)}, bf16[2,2,1152,128]{2,3,0,1:T(8,128)(2,1)}, u32[]{:S(2)}, u32[]{:S(2)}) collective-permute-start(bf16[2,2,1152,128]{2,3,0,1:T(8,128)(2,1)} %get-tuple-element.44), channel_id=1, source_target_pairs={{24,16},{25,17},{26,18},{27,19},{28,20},{29,21},{30,22},{31,23}} | collective-permute-start | bytes 3538952 | tf_op jit(solution)/shard_map/ppermute | solution.py:24
  745.5 109.7 %collective-permute-start.6 = (bf16[2,2,1152,128]{2,3,0,1:T(8,128)(2,1)}, bf16[2,2,1152,128]{2,3,0,1:T(8,128)(2,1)}, u32[]{:S(2)}, u32[]{:S(2)}) collective-permute-start(bf16[2,2,1152,128]{2,3,0,1:T(8,128)(2,1)} %get-tuple-element.47), channel_id=1, source_target_pairs={{0,8},{1,9},{2,10},{3,11},{4,12},{5,13},{6,14},{7,15}} | collective-permute-start | bytes 3538952 | tf_op jit(solution)/shard_map/ppermute | solution.py:24
  851.2 32.7 %collective-permute-start.12 = (bf16[2,2,1152,128]{2,3,0,1:T(8,128)(2,1)S(1)}, bf16[2,2,1152,128]{2,3,0,1:T(8,128)(2,1)S(1)}, u32[]{:S(2)}, u32[]{:S(2)}) collective-permute-start(bf16[2,2,1152,128]{2,3,0,1:T(8,128)(2,1)S(1)} %get-tuple-element.51), channel_id=1, source_target_pairs={{0,8},{1,9},{2,10},{3,11},{4,12},{5,13},{6,14},{7,15}} | collective-permute-start | bytes 3538952 | tf_op jit(solution)/shard_map/ppermute | solution.py:24
  855.2 54.0 %collective-permute-start.19 = (bf16[2,2,1152,128]{2,3,0,1:T(8,128)(2,1)S(1)}, bf16[2,2,1152,128]{2,3,0,1:T(8,128)(2,1)S(1)}, u32[]{:S(2)}, u32[]{:S(2)}) collective-permute-start(bf16[2,2,1152,128]{2,3,0,1:T(8,128)(2,1)S(1)} %fusion.24), channel_id=1, source_target_pairs={{0,8},{8,16},{1,9},{9,17},{2,10},{10,18},{3,11},{11,19},{4,12},{12... | collective-permute-start | bytes 3538952 | tf_op jit(solution)/shard_map/ppermute | solution.py:24
  860.9 80.2 %collective-permute-start.9 = (bf16[2,2,1152,128]{2,3,0,1:T(8,128)(2,1)S(1)}, bf16[2,2,1152,128]{2,3,0,1:T(8,128)(2,1)}, u32[]{:S(2)}, u32[]{:S(2)}) collective-permute-start(bf16[2,2,1152,128]{2,3,0,1:T(8,128)(2,1)S(1)} %get-tuple-element.48), channel_id=1, source_target_pairs={{24,16},{25,17},{26,18},{27,19},{28,20},{29,21},{30,22},{31,23}} | collective-permute-start | bytes 3538952 | tf_op jit(solution)/shard_map/ppermute | solution.py:24
  883.9 50.6 %collective-permute-start.1 = (bf16[2,2,1152,128]{2,3,0,1:T(8,128)(2,1)S(1)}, bf16[2,2,1152,128]{2,3,0,1:T(8,128)(2,1)S(1)}, u32[]{:S(2)}, u32[]{:S(2)}) collective-permute-start(bf16[2,2,1152,128]{2,3,0,1:T(8,128)(2,1)S(1)} %fusion.36), channel_id=1, source_target_pairs={{0,8},{8,16},{1,9},{9,17},{2,10},{10,18},{3,11},{11,19},{4,12},{12... | collective-permute-start | bytes 3538952 | tf_op jit(solution)/shard_map/ppermute | solution.py:24
  886.1 79.0 %collective-permute-start.15 = (bf16[2,2,1152,128]{2,3,0,1:T(8,128)(2,1)S(1)}, bf16[2,2,1152,128]{2,3,0,1:T(8,128)(2,1)S(1)}, u32[]{:S(2)}, u32[]{:S(2)}) collective-permute-start(bf16[2,2,1152,128]{2,3,0,1:T(8,128)(2,1)S(1)} %get-tuple-element.52), channel_id=1, source_target_pairs={{24,16},{25,17},{26,18},{27,19},{28,20},{29,21},{30,22},{31,23}} | collective-permute-start | bytes 3538952 | tf_op jit(solution)/shard_map/ppermute | solution.py:24
  910.2 49.6 %collective-permute-start.7 = (bf16[2,2,1152,128]{2,3,0,1:T(8,128)(2,1)S(1)}, bf16[2,2,1152,128]{2,3,0,1:T(8,128)(2,1)}, u32[]{:S(2)}, u32[]{:S(2)}) collective-permute-start(bf16[2,2,1152,128]{2,3,0,1:T(8,128)(2,1)S(1)} %fusion.32), channel_id=1, source_target_pairs={{0,8},{8,16},{1,9},{9,17},{2,10},{10,18},{3,11},{11,19},{4,12},{12... | collective-permute-start | bytes 3538952 | tf_op jit(solution)/shard_map/ppermute | solution.py:24
  916.7 68.4 %collective-permute-start.13 = (bf16[2,2,1152,128]{2,3,0,1:T(8,128)(2,1)S(1)}, bf16[2,2,1152,128]{2,3,0,1:T(8,128)(2,1)}, u32[]{:S(2)}, u32[]{:S(2)}) collective-permute-start(bf16[2,2,1152,128]{2,3,0,1:T(8,128)(2,1)S(1)} %fusion.28), channel_id=1, source_target_pairs={{0,8},{8,16},{1,9},{9,17},{2,10},{10,18},{3,11},{11,19},{4,12},{12... | collective-permute-start | bytes 3538952 | tf_op jit(solution)/shard_map/ppermute | solution.py:24
  935.5 113.4 %collective-permute-start.20 = (bf16[2,2,1152,128]{2,3,0,1:T(8,128)(2,1)S(1)}, bf16[2,2,1152,128]{2,3,0,1:T(8,128)(2,1)S(1)}, u32[]{:S(2)}, u32[]{:S(2)}) collective-permute-start(bf16[2,2,1152,128]{2,3,0,1:T(8,128)(2,1)S(1)} %get-tuple-element.53), channel_id=1, source_target_pairs={{0,8},{8,16},{16,24},{1,9},{9,17},{17,25},{2,10},{10,18},{18,26},{... | collective-permute-start | bytes 3538952 | tf_op jit(solution)/shard_map/ppermute | solution.py:24
  941.2 48.6 %collective-permute-start.22 = (bf16[2,2,1152,128]{2,3,0,1:T(8,128)(2,1)}, bf16[2,2,1152,128]{2,3,0,1:T(8,128)(2,1)S(1)}, u32[]{:S(2)}, u32[]{:S(2)}) collective-permute-start(bf16[2,2,1152,128]{2,3,0,1:T(8,128)(2,1)} %get-tuple-element.54), channel_id=1, source_target_pairs={{24,16},{16,8},{25,17},{17,9},{26,18},{18,10},{27,19},{19,11},{28,... | collective-permute-start | bytes 3538952 | tf_op jit(solution)/shard_map/ppermute | solution.py:24
  959.9 116.3 %collective-permute-start.2 = (bf16[2,2,1152,128]{2,3,0,1:T(8,128)(2,1)}, bf16[2,2,1152,128]{2,3,0,1:T(8,128)(2,1)S(1)}, u32[]{:S(2)}, u32[]{:S(2)}) collective-permute-start(bf16[2,2,1152,128]{2,3,0,1:T(8,128)(2,1)} %get-tuple-element.41), channel_id=1, source_target_pairs={{0,8},{8,16},{16,24},{1,9},{9,17},{17,25},{2,10},{10,18},{18,26},{... | collective-permute-start | bytes 3538952 | tf_op jit(solution)/shard_map/ppermute | solution.py:24
  965.1 58.4 %collective-permute-start.4 = (bf16[2,2,1152,128]{2,3,0,1:T(8,128)(2,1)}, bf16[2,2,1152,128]{2,3,0,1:T(8,128)(2,1)S(1)}, u32[]{:S(2)}, u32[]{:S(2)}) collective-permute-start(bf16[2,2,1152,128]{2,3,0,1:T(8,128)(2,1)} %get-tuple-element.42), channel_id=1, source_target_pairs={{24,16},{16,8},{25,17},{17,9},{26,18},{18,10},{27,19},{19,11},{28,... | collective-permute-start | bytes 3538952 | tf_op jit(solution)/shard_map/ppermute | solution.py:24
  985.1 36.2 %collective-permute-start.10 = (bf16[2,2,1152,128]{2,3,0,1:T(8,128)(2,1)}, bf16[2,2,1152,128]{2,3,0,1:T(8,128)(2,1)S(1)}, u32[]{:S(2)}, u32[]{:S(2)}) collective-permute-start(bf16[2,2,1152,128]{2,3,0,1:T(8,128)(2,1)} %get-tuple-element.46), channel_id=1, source_target_pairs={{24,16},{16,8},{25,17},{17,9},{26,18},{18,10},{27,19},{19,11},{28,... | collective-permute-start | bytes 3538952 | tf_op jit(solution)/shard_map/ppermute | solution.py:24
  989.8 56.9 %collective-permute-start.16 = (bf16[2,2,1152,128]{2,3,0,1:T(8,128)(2,1)}, bf16[2,2,1152,128]{2,3,0,1:T(8,128)(2,1)S(1)}, u32[]{:S(2)}, u32[]{:S(2)}) collective-permute-start(bf16[2,2,1152,128]{2,3,0,1:T(8,128)(2,1)} %get-tuple-element.50), channel_id=1, source_target_pairs={{24,16},{16,8},{25,17},{17,9},{26,18},{18,10},{27,19},{19,11},{28,... | collective-permute-start | bytes 3538952 | tf_op jit(solution)/shard_map/ppermute | solution.py:24
  1021.4 50.6 %collective-permute-start.23 = (bf16[2,2,1152,128]{2,3,0,1:T(8,128)(2,1)S(1)}, bf16[2,2,1152,128]{2,3,0,1:T(8,128)(2,1)S(1)}, u32[]{:S(2)}, u32[]{:S(2)}) collective-permute-start(bf16[2,2,1152,128]{2,3,0,1:T(8,128)(2,1)S(1)} %fusion.23), channel_id=1, source_target_pairs={{24,16},{16,8},{8,0},{25,17},{17,9},{9,1},{26,18},{18,10},{10,2},{... | collective-permute-start | bytes 3538952 | tf_op jit(solution)/shard_map/ppermute | solution.py:24
  1023.5 75.7 %collective-permute-start.8 = (bf16[2,2,1152,128]{2,3,0,1:T(8,128)(2,1)S(1)}, bf16[2,2,1152,128]{2,3,0,1:T(8,128)(2,1)S(1)}, u32[]{:S(2)}, u32[]{:S(2)}) collective-permute-start(bf16[2,2,1152,128]{2,3,0,1:T(8,128)(2,1)S(1)} %get-tuple-element.45), channel_id=1, source_target_pairs={{0,8},{8,16},{16,24},{1,9},{9,17},{17,25},{2,10},{10,18},{18,26},{... | collective-permute-start | bytes 3538952 | tf_op jit(solution)/shard_map/ppermute | solution.py:24
  1046.6 50.6 %collective-permute-start.5 = (bf16[2,2,1152,128]{2,3,0,1:T(8,128)(2,1)S(1)}, bf16[2,2,1152,128]{2,3,0,1:T(8,128)(2,1)S(1)}, u32[]{:S(2)}, u32[]{:S(2)}) collective-permute-start(bf16[2,2,1152,128]{2,3,0,1:T(8,128)(2,1)S(1)} %fusion.35), channel_id=1, source_target_pairs={{24,16},{16,8},{8,0},{25,17},{17,9},{9,1},{26,18},{18,10},{10,2},{... | collective-permute-start | bytes 3538952 | tf_op jit(solution)/shard_map/ppermute | solution.py:24
  1048.9 74.0 %collective-permute-start.14 = (bf16[2,2,1152,128]{2,3,0,1:T(8,128)(2,1)S(1)}, bf16[2,2,1152,128]{2,3,0,1:T(8,128)(2,1)S(1)}, u32[]{:S(2)}, u32[]{:S(2)}) collective-permute-start(bf16[2,2,1152,128]{2,3,0,1:T(8,128)(2,1)S(1)} %copy-done.14), channel_id=1, source_target_pairs={{0,8},{8,16},{16,24},{1,9},{9,17},{17,25},{2,10},{10,18},{18,26},{... | collective-permute-start | bytes 3538952 | tf_op jit(solution)/shard_map/ppermute | solution.py:24
  1071.9 50.6 %collective-permute-start.11 = (bf16[2,2,1152,128]{2,3,0,1:T(8,128)(2,1)S(1)}, bf16[2,2,1152,128]{2,3,0,1:T(8,128)(2,1)S(1)}, u32[]{:S(2)}, u32[]{:S(2)}) collective-permute-start(bf16[2,2,1152,128]{2,3,0,1:T(8,128)(2,1)S(1)} %fusion.31), channel_id=1, source_target_pairs={{24,16},{16,8},{8,0},{25,17},{17,9},{9,1},{26,18},{18,10},{10,2},{... | collective-permute-start | bytes 3538952 | tf_op jit(solution)/shard_map/ppermute | solution.py:24
  1076.1 69.9 %collective-permute-start.17 = (bf16[2,2,1152,128]{2,3,0,1:T(8,128)(2,1)S(1)}, bf16[2,2,1152,128]{2,3,0,1:T(8,128)(2,1)S(1)}, u32[]{:S(2)}, u32[]{:S(2)}) collective-permute-start(bf16[2,2,1152,128]{2,3,0,1:T(8,128)(2,1)S(1)} %fusion.27), channel_id=1, source_target_pairs={{24,16},{16,8},{8,0},{25,17},{17,9},{9,1},{26,18},{18,10},{10,2},{... | collective-permute-start | bytes 3538952 | tf_op jit(solution)/shard_map/ppermute | solution.py:24
  (27 other events, 626.1 us)
Sparse Core Ops, SparseCore 0:
  66.8 117.1 reduce-scatter.8
  187.5 115.9 reduce-scatter.10
  307.0 115.9 reduce-scatter.6
  426.4 115.9 reduce-scatter.4
  556.5 54.4 all-gather.14
  612.7 54.3 all-gather.8
  669.0 54.3 all-gather.10
  725.3 54.3 all-gather.12
